TPU v7x, 32 devices: a whole 2x2x4 slice. The times are simulated.
32 devices in a mesh: grp: 2 (over y), freq: 8 (over z, x), site: 2 (over core).
Axes of the slice: x: 2, y: 2, z: 4, core: 2. Of those that a mesh axis runs over, the one named last changes fastest.
Arguments:
- green: bfloat16 [8, 1024, 8, 3, 2, 128], P('freq', None, ('grp', 'site')), parts along dimension 2, may hold values from -0.1875 to 0.1875
- slip: bfloat16 [8, 16, 8, 128], P(None, 'site'), may hold values from 0.099609375 to 1
- positions: float32 [3, 1024], replicated, may hold values from 0 to 40
- hypocenters: float32 [8, 4, 3], replicated, may hold values from 0 to 40
- slowness: float32 [8, 4], replicated, may hold values from 1 to 3
- rise: float32 [8, 16], replicated, may hold values from 0.5 to 6
- block_lists: int32 [8, 8], replicated, may hold values from 0 to 7, as said below
- block_counts: int32 [8], replicated, may hold values from 1 to 8, 48 in all
- var_counts: int32 [8], replicated, may hold values from 1 to 64, as said below
- region_map: int32 [8], replicated, may hold values from 0 to 7, each once
Outputs:
- seismograms: float32 [512, 8, 3, 2048], P('freq', ('grp', 'site')), parts along dimension 1
There are 2 independent parts, one for each index of `grp`. A program takes and returns all parts, laid end to end along the dimension named above; an argument that names none is the same for every part. Nothing has to cross between parts.
Inputs may be any that keep to these rules, and one draw needn't show every extreme that they name: `block_lists`: rupture r lists consecutive blocks s_r, s_r + 1, ... modulo 8; only its first block_counts[r] entries are used. `block_counts`: the counts sum to 48. Variations 0 .. var_counts[r] - 1 of rupture r are live. `region_map`: each row appears once.
All inputs are finite; a program needn't handle non-finite values.
Results may differ from a plain program's by a relative error of at most 0.0048.
Values may be sent and summed in bfloat16 or wider, within the bound.
A program may use at most 192 MiB of HBM per device.

v0:
```python
import math
import jax
import jax.numpy as jnp
from jax import lax
from jax.sharding import PartitionSpec as P

F = 1024
C = 3
TWO_PI = 2.0 * math.pi
OUT_GAIN = 8.0


def on_device(
    green,
    slip,
    positions,
    hypocenters,
    slowness,
    rise,
    block_lists,
    block_counts,
    var_counts,
    region_map,
):
    freq_count = lax.axis_size("freq")
    fdev_bins = green.shape[1] // freq_count
    point_count = green.shape[-1]
    rupture_count = block_lists.shape[0]
    list_len = block_lists.shape[1]
    hypo_count = hypocenters.shape[1]
    wave_len = 2 * F
    slip_all = lax.all_gather(slip, "site", axis=1, tiled=True)
    real_count = slip_all.shape[1]
    first_bin = lax.axis_index("freq") * fdev_bins
    local_bins = first_bin + jnp.arange(fdev_bins, dtype=jnp.int32)
    omegas = TWO_PI * local_bins.astype(jnp.float32) / wave_len
    points_all = positions.reshape(3, positions.shape[1] // point_count, point_count)
    slot_total = rupture_count * list_len
    slot_index = jnp.arange(slot_total, dtype=jnp.int32)
    slot_rup = slot_index // list_len
    slot_pos = slot_index % list_len
    slot_live = slot_pos < block_counts[slot_rup]
    group_size = math.gcd(slot_total, 32)
    turn_count = slot_total // group_size
    rupture_ids = jnp.arange(rupture_count, dtype=jnp.int32)
    tiles_here = lax.all_to_all(green, "freq", split_axis=1, concat_axis=0, tiled=True)
    site_items = tiles_here.shape[2]

    def one_turn(turn_index, totals):
        start = turn_index * group_size
        group_rup = lax.dynamic_slice_in_dim(slot_rup, start, group_size)
        group_pos = lax.dynamic_slice_in_dim(slot_pos, start, group_size)
        group_live = lax.dynamic_slice_in_dim(slot_live, start, group_size)
        blocks = block_lists[group_rup, group_pos]
        tile = tiles_here[region_map[blocks]].astype(jnp.float32)
        points = points_all[:, blocks, :].transpose(1, 0, 2)
        centers = hypocenters[group_rup]
        slows = slowness[group_rup]
        sq_dist = jnp.sum((points[:, None, :, :] - centers[:, :, :, None]) ** 2, axis=2)
        onset_time = slows[:, :, None] * jnp.sqrt(sq_dist)
        phases = omegas[None, None, :, None] * onset_time[:, :, None, :]
        wave_re = jnp.cos(phases)[:, :, :, None, None, :]
        wave_im = -jnp.sin(phases)[:, :, :, None, None, :]
        tile_re = tile[:, None, :, :, :, 0, :]
        tile_im = tile[:, None, :, :, :, 1, :]
        weighted = jnp.stack(
            [wave_re * tile_re - wave_im * tile_im, wave_re * tile_im + wave_im * tile_re], axis=5
        ).astype(jnp.bfloat16)
        amps = slip_all[group_rup, :, group_pos]
        amps = jnp.where(group_live[:, None, None], amps, jnp.zeros_like(amps))
        onehot = (group_rup[None, :] == rupture_ids[:, None]).astype(jnp.bfloat16)
        routed = onehot[:, :, None, None] * amps[None, :, :, :]
        term = jnp.einsum(
            "rgkp,ghfscqp->rkhfscq", routed, weighted, preferred_element_type=jnp.float32
        )
        return totals + term

    start_totals = jnp.zeros(
        (rupture_count, real_count, hypo_count, fdev_bins, site_items, C, 2), jnp.float32
    )
    totals = lax.fori_loop(0, turn_count, one_turn, start_totals)
    ratio = omegas[None, None, :] * rise[:, :, None]
    denom = 1.0 + ratio * ratio
    stf_re = (1.0 / denom)[:, :, None, :, None, None]
    stf_im = (-ratio / denom)[:, :, None, :, None, None]
    part_re = totals[..., 0]
    part_im = totals[..., 1]
    spec_re = stf_re * part_re - stf_im * part_im
    spec_im = stf_re * part_im + stf_im * part_re
    spectrum = jnp.stack([spec_re, spec_im], axis=-1).transpose(0, 1, 2, 4, 5, 6, 3)
    variation = (
        jnp.arange(real_count, dtype=jnp.int32)[:, None] * hypo_count
        + jnp.arange(hypo_count, dtype=jnp.int32)[None, :]
    )
    live = variation[None, :, :] < var_counts[:, None, None]
    spectrum = jnp.where(live[:, :, :, None, None, None, None], spectrum, jnp.zeros_like(spectrum))
    spectrum = spectrum.reshape(
        rupture_count * real_count * hypo_count, site_items, C, 2, fdev_bins
    ).astype(jnp.bfloat16)
    own_rows = lax.all_to_all(spectrum, "freq", split_axis=0, concat_axis=4, tiled=True)
    row_count = own_rows.shape[0]
    site_count = own_rows.shape[1]
    spec_rows = own_rows.reshape(row_count * site_count * C, 2 * F)
    bins = jnp.arange(F, dtype=jnp.int32)
    piece_len = min(512, wave_len)
    pieces = []
    for piece_index in range(wave_len // piece_len):
        samples = piece_index * piece_len + jnp.arange(piece_len, dtype=jnp.int32)
        products = bins[:, None] * samples[None, :] % wave_len
        angles = TWO_PI * products.astype(jnp.float32) / wave_len
        wave_table = jnp.concatenate([jnp.cos(angles), -jnp.sin(angles)], axis=0).astype(
            jnp.bfloat16
        )
        pieces.append(
            jnp.dot(spec_rows, wave_table, preferred_element_type=jnp.float32)
            * (OUT_GAIN / math.sqrt(F))
        )
    motion = jnp.concatenate(pieces, axis=1)
    return motion.reshape(row_count, site_count, C, wave_len)


def solution(mesh):
    placed = (
        P("freq", None, ("grp", "site"), None, None, None),
        P(None, "site", None, None),
        P(),
        P(),
        P(),
        P(),
        P(),
        P(),
        P(),
        P(),
    )
    return jax.shard_map(
        on_device,
        mesh=mesh,
        in_specs=placed,
        out_specs=P("freq", ("grp", "site"), None, None),
        check_vma=False,
    )
```

profile of v0, /device:TPU:0, one launch (start us, length us, event | category | flops | bytes accessed | tf_op | source)
XLA Modules:
  0.0 425.7 jit_solution(9974423023385828386)
XLA Ops:
  0.0 7.4 %all-to-all-start = ((bf16[1,1024,2,3,2,128]{5,4,3,2,0,1:T(2,128)(2,1)}), bf16[1,1024,2,3,2,128]{5,4,3,2,0,1:T(2,128)(2,1)S(1)}, u32[]{:S(2)}, u32[]{:S(2)}) async-start(bf16[1,1024,2,3,2,128]{5,4,3,2,0,1:T(2,128)(2,1)} %bitcast.80), calls=%async_computation | async-start | bytes 6291456 | tf_op jit(solution)/shard_map/all_to_all | solution.py:46
  7.5 0.1 copy.70
  7.7 2.1 all_gather.3
  9.9 0.7 fusion.80
  10.6 5.2 %fusion.75 = pred[64]{0:T(512)(128)(4,1)S(1)} fusion(s32[]{:T(128)} %bitcast.2, s32[]{:T(128)} %bitcast.3, s32[]{:T(128)} %bitcast.4, s32[]{:T(128)} %bitcast.5, s32[]{:T(128)} %bitcast.6, s32[]{:T(128)} %bitcast.8, s32[]{:T(128)} %bitcast.7, s32[]{:T(128)} %bitcast.1), kind=kLoop, calls=%fused_computation.141 | loop fusion | flops 2048 | bytes 96 | tf_op jit(solution)/shard_map/lt | solution.py:42
  15.8 0.7 broadcast_compare_fusion
  16.4 0.7 fusion.73
  17.2 61.0 %all-to-all-done = bf16[1,1024,2,3,2,128]{5,4,3,2,0,1:T(2,128)(2,1)S(1)} async-done(((bf16[1,1024,2,3,2,128]{5,4,3,2,0,1:T(2,128)(2,1)}), bf16[1,1024,2,3,2,128]{5,4,3,2,0,1:T(2,128)(2,1)S(1)}, u32[]{:S(2)}, u32[]{:S(2)}) %all-to-all-start) | async-done | bytes 3145760 | tf_op jit(solution)/shard_map/all_to_all | solution.py:46
  78.2 1.6 copy-done.2
  79.8 2.8 copy.71
  82.7 275.0 %while.14 = (s32[]{:T(128)}, f32[8,16,4,128,2,3,2]{3,1,6,5,4,2,0:T(8,128)}, s32[64]{0:T(128)S(1)}, pred[64]{0:T(512)(128)(4,1)S(1)}, s32[64]{0:T(128)S(1)}, /*in...) while((s32[]{:T(128)}, ...), condition=%wide.region_2.3_spmd.clone, body=%wide.region_0.2_spmd.clone.sunk | while | flops 6658150912 | bytes 280112832 | solution.py:81
  82.8 0.7 gather_fusion.1
  83.5 0.6 gather_fusion.2
  84.2 0.6 gather_fusion
  84.8 0.1 copy.93
  84.9 0.1 multiply_reduce_fusion.2
  85.0 0.6 gather_fusion.3
  85.7 0.1 sqrt_multiply_fusion.2
  85.8 32.0 %multiply_cosine_fusion.2 = (f32[32,4,128,128]{3,2,0,1:T(8,128)}, f32[32,4,128,128]{3,2,0,1:T(8,128)}) fusion(f32[32,4,128]{2,0,1:T(8,128)S(1)} %sqrt_multiply_fusion.2, f32[128]{0:T(128)S(1)} %convert_multiply_fusion.3), kind=kLoop, calls=%fused_computation.16.clone.1 | loop fusion | flops 4194304 | bytes 16843264 | tf_op jit(solution)/shard_map/while/body/eval_jaxpr/cos | solution.py:62
  117.7 0.7 gather_fusion.4
  118.5 6.8 %gather_fusion.5 = bf16[32,128,2,3,2,128]{5,1,4,3,2,0:T(8,128)(2,1)} fusion(bf16[8,128,2,3,2,128]{5,1,4,3,2,0:T(8,128)(2,1)S(1)} %get-tuple-element.556, s32[1024]{0:T(1024)S(1)} %pad_clamp_fusion.8), kind=kCustom, calls=%fused_computation.6.clone.clone.1 | custom fusion | bytes 25165952 | tf_op jit(solution)/shard_map/while/body/eval_jaxpr/gather | solution.py:55
  125.3 14.4 %convert_element_type.116 = f32[32,128,2,3,2,128]{5,1,4,3,2,0:T(8,128)} convert(bf16[32,128,2,3,2,128]{5,1,4,3,2,0:T(8,128)(2,1)} %gather_fusion.5) | non-fusion elementwise | flops 6291456 | bytes 37748736 | tf_op jit(solution)/shard_map/while/body/eval_jaxpr/convert_element_type | solution.py:55
  139.7 14.2 %slice_bitcast_fusion.3 = (f32[32,128,2,3,128]{4,1,3,2,0:T(8,128)S(1)}, f32[32,128,2,3,128]{4,1,3,2,0:T(8,128)}) fusion(f32[32,128,2,3,2,128]{5,1,4,3,2,0:T(8,128)} %convert_element_type.116), kind=kLoop, calls=%fused_computation.14.clone.1 | loop fusion | bytes 50331648 | tf_op jit(solution)/shard_map/while/body/eval_jaxpr/mul | solution.py:67
  153.9 41.2 %subtract_convert_fusion.2 = (bf16[32,4,128,2,3,1,128]{6,2,0,5,4,3,1:T(8,128)(2,1)}, bf16[32,4,128,2,3,1,128]{6,2,0,5,4,3,1:T(8,128)(2,1)}) fusion(f32[32,4,128,128]{3,2,0,1:T(8,128)} %get-tuple-element.505, f32[32,4,128,128]{3,2,0,1:T(8,128)} %get-tuple-element.506, f32[32,128,2,3,128]{4,1,3,2,0:T(8,128)S(1)} %get-tuple-element.507, ...), kind=kLoop, calls=%fused_computation.11.clone.1 | loop fusion | flops 100663296 | bytes 92274688 | tf_op jit(solution)/shard_map/convert
  195.1 1.6 gather_fusion.6
  196.8 0.1 broadcast_select_fusion.2
  196.9 23.2 %bitcast_add_fusion.2 = f32[8,16,4,128,2,3,2]{3,1,6,5,4,2,0:T(8,128)} fusion(f32[8,16,4,128,2,3,2]{3,1,6,5,4,2,0:T(8,128)} %get-tuple-element.529, bf16[32,4,128,2,3,1,128]{6,2,0,5,4,3,1:T(8,128)(2,1)} %get-tuple-element.509, bf16[32,4,128,2,3,1,128]{6,2,0,5,4,3,1:T(8,128)(2,1)} %get-tuple-element.510, pred[]{:T(512)S(6)} %compare.103, ...), kind=kOutput, calls=%fused_computation.18.clone.1 | convolution fusion | flops 6546784256 | bytes 56754688 | tf_op jit(solution)/shard_map/while/body/eval_jaxpr/rgkp,ghfscqp->rkhfscq/dot_general | solution.py:73
  220.2 0.7 gather_fusion.1
  220.9 0.6 gather_fusion.2
  221.5 0.6 gather_fusion
  222.1 0.1 copy.93
  222.2 0.1 multiply_reduce_fusion.2
  222.4 0.6 gather_fusion.3
  223.1 32.0 %multiply_cosine_fusion.2 = (f32[32,4,128,128]{3,2,0,1:T(8,128)}, f32[32,4,128,128]{3,2,0,1:T(8,128)}) fusion(f32[32,4,128]{2,0,1:T(8,128)S(1)} %sqrt_multiply_fusion.2, f32[128]{0:T(128)S(1)} %convert_multiply_fusion.3), kind=kLoop, calls=%fused_computation.16.clone.1 | loop fusion | flops 4194304 | bytes 16843264 | tf_op jit(solution)/shard_map/while/body/eval_jaxpr/cos | solution.py:62
  255.1 0.7 gather_fusion.4
  255.8 6.8 %gather_fusion.5 = bf16[32,128,2,3,2,128]{5,1,4,3,2,0:T(8,128)(2,1)} fusion(bf16[8,128,2,3,2,128]{5,1,4,3,2,0:T(8,128)(2,1)S(1)} %get-tuple-element.556, s32[1024]{0:T(1024)S(1)} %pad_clamp_fusion.8), kind=kCustom, calls=%fused_computation.6.clone.clone.1 | custom fusion | bytes 25165952 | tf_op jit(solution)/shard_map/while/body/eval_jaxpr/gather | solution.py:55
  262.6 14.4 %convert_element_type.116 = f32[32,128,2,3,2,128]{5,1,4,3,2,0:T(8,128)} convert(bf16[32,128,2,3,2,128]{5,1,4,3,2,0:T(8,128)(2,1)} %gather_fusion.5) | non-fusion elementwise | flops 6291456 | bytes 37748736 | tf_op jit(solution)/shard_map/while/body/eval_jaxpr/convert_element_type | solution.py:55
  277.0 14.2 %slice_bitcast_fusion.3 = (f32[32,128,2,3,128]{4,1,3,2,0:T(8,128)S(1)}, f32[32,128,2,3,128]{4,1,3,2,0:T(8,128)}) fusion(f32[32,128,2,3,2,128]{5,1,4,3,2,0:T(8,128)} %convert_element_type.116), kind=kLoop, calls=%fused_computation.14.clone.1 | loop fusion | bytes 50331648 | tf_op jit(solution)/shard_map/while/body/eval_jaxpr/mul | solution.py:67
  291.2 41.2 %subtract_convert_fusion.2 = (bf16[32,4,128,2,3,1,128]{6,2,0,5,4,3,1:T(8,128)(2,1)}, bf16[32,4,128,2,3,1,128]{6,2,0,5,4,3,1:T(8,128)(2,1)}) fusion(f32[32,4,128,128]{3,2,0,1:T(8,128)} %get-tuple-element.505, f32[32,4,128,128]{3,2,0,1:T(8,128)} %get-tuple-element.506, f32[32,128,2,3,128]{4,1,3,2,0:T(8,128)S(1)} %get-tuple-element.507, ...), kind=kLoop, calls=%fused_computation.11.clone.1 | loop fusion | flops 100663296 | bytes 92274688 | tf_op jit(solution)/shard_map/convert
  332.4 1.6 gather_fusion.6
  334.1 0.1 broadcast_select_fusion.2
  334.2 23.5 %bitcast_add_fusion.2 = f32[8,16,4,128,2,3,2]{3,1,6,5,4,2,0:T(8,128)} fusion(f32[8,16,4,128,2,3,2]{3,1,6,5,4,2,0:T(8,128)} %get-tuple-element.529, bf16[32,4,128,2,3,1,128]{6,2,0,5,4,3,1:T(8,128)(2,1)} %get-tuple-element.509, bf16[32,4,128,2,3,1,128]{6,2,0,5,4,3,1:T(8,128)(2,1)} %get-tuple-element.510, pred[]{:T(512)S(6)} %compare.103, ...), kind=kOutput, calls=%fused_computation.18.clone.1 | convolution fusion | flops 6546784256 | bytes 56754688 | tf_op jit(solution)/shard_map/while/body/eval_jaxpr/rgkp,ghfscqp->rkhfscq/dot_general | solution.py:73
  357.7 2.4 multiply_subtract_fusion
  360.1 0.4 fusion.58
  360.5 2.0 copy.72
  362.5 2.8 copy.73
  365.3 3.6 all-to-all-start.1
  368.9 9.3 %negate_convert_fusion.3 = (bf16[1024,512]{1,0:T(8,128)(2,1)}, bf16[1024,512]{1,0:T(8,128)(2,1)}) fusion(), kind=kLoop, calls=%fused_computation.97 | loop fusion | flops 8912896 | bytes 2097152 | tf_op jit(solution)/shard_map/convert.9
  378.2 9.4 %cosine_convert_fusion.1 = (bf16[1024,512]{1,0:T(8,128)(2,1)}, bf16[1024,512]{1,0:T(8,128)(2,1)}) fusion(s32[512]{0:T(512)S(1)} %iota_add_fusion.1), kind=kLoop, calls=%fused_computation.90 | loop fusion | flops 8912896 | bytes 2099200 | tf_op jit(solution)/shard_map/convert.4
  387.6 9.4 %cosine_convert_fusion.2 = (bf16[1024,512]{1,0:T(8,128)(2,1)}, bf16[1024,512]{1,0:T(8,128)(2,1)}) fusion(s32[512]{0:T(512)S(1)} %iota_add_fusion.2), kind=kLoop, calls=%fused_computation.94 | loop fusion | flops 8912896 | bytes 2099200 | tf_op jit(solution)/shard_map/convert.6
  397.0 9.3 %cosine_convert_fusion = (bf16[1024,512]{1,0:T(8,128)(2,1)}, bf16[1024,512]{1,0:T(8,128)(2,1)}) fusion(s32[512]{0:T(512)S(1)} %iota_add_fusion), kind=kLoop, calls=%fused_computation.86 | loop fusion | flops 8912896 | bytes 2099200 | tf_op jit(solution)/shard_map/convert.2
  406.3 1.8 copy.85
  408.2 0.7 reshape.209
  408.9 2.7 fusion.62
  411.6 1.0 fusion.65
  412.6 0.2 copy-done.8
  412.8 0.3 copy-done.9
  413.2 1.0 fusion.68
  414.2 0.2 copy-done.4
  414.4 0.3 copy-done.5
  414.7 1.0 fusion.59
  415.7 0.3 pad_maximum_fusion
  416.0 3.0 reshape.210
  419.0 6.8 %copy.75 = f32[64,2,3,2048]{3,1,2,0:T(2,128)} copy(f32[64,2,3,2048]{3,2,1,0:T(4,128)} %reshape.210) | data formatting | bytes 6291456 | tf_op jit(solution)/shard_map/reshape | solution.py:119
  (65 shorter events, 1.0 us)
Async XLA Ops:
  0.0 7.5 %copy-start.10 = (bf16[8,8,8,128]{3,2,1,0:T(8,128)(2,1)S(1)}, bf16[8,8,8,128]{3,2,1,0:T(8,128)(2,1)}, u32[]{:S(2)}) copy-start(bf16[8,8,8,128]{3,2,1,0:T(8,128)(2,1)} %param.13) | copy-start | bytes 393220
  0.0 7.5 %copy-start.13 = (f32[8,4,3]{0,1,2:T(4,128)S(1)}, f32[8,4,3]{0,1,2:T(4,128)}, u32[]{:S(2)}) copy-start(f32[8,4,3]{0,1,2:T(4,128)} %param.15) | copy-start | bytes 1156
  0.0 7.6 %copy-start.15 = (f32[8,4]{0,1:T(4,128)S(1)}, f32[8,4]{0,1:T(4,128)}, u32[]{:S(2)}) copy-start(f32[8,4]{0,1:T(4,128)} %param.16) | copy-start | bytes 388
  0.0 9.8 %copy-start.11 = (s32[8]{0:T(128)S(1)}, s32[8]{0:T(128)}, u32[]{:S(2)}) copy-start(s32[8]{0:T(128)} %param.19) | copy-start | bytes 100
  0.0 15.7 %copy-start.16 = (s32[8]{0:T(128)S(1)}, s32[8]{0:T(128)}, u32[]{:S(2)}) copy-start(s32[8]{0:T(128)} %param.20) | copy-start | bytes 100
  0.0 16.4 %copy-start.14 = (f32[8,16]{1,0:T(8,128)S(1)}, f32[8,16]{1,0:T(8,128)}, u32[]{:S(2)}) copy-start(f32[8,16]{1,0:T(8,128)} %param.17) | copy-start | bytes 1540
  0.0 78.1 %all-to-all-start = ((bf16[1,1024,2,3,2,128]{5,4,3,2,0,1:T(2,128)(2,1)}), bf16[1,1024,2,3,2,128]{5,4,3,2,0,1:T(2,128)(2,1)S(1)}, u32[]{:S(2)}, u32[]{:S(2)}) async-start(bf16[1,1024,2,3,2,128]{5,4,3,2,0,1:T(2,128)(2,1)} %bitcast.80), calls=%async_computation | async-start | bytes 6291456 | tf_op jit(solution)/shard_map/all_to_all | solution.py:46
  78.2 1.6 copy-start.2
  79.8 2.8 copy-start
  79.8 2.8 copy-start.1
  79.8 2.8 copy-start.3
  357.7 2.4 copy-start.12
  365.3 41.1 %all-to-all-start.1 = ((bf16[512,2,3,2,128]{4,3,2,1,0:T(2,128)(2,1)}), bf16[512,2,3,2,128]{4,3,2,1,0:T(2,128)(2,1)S(1)}, u32[]{:S(2)}, u32[]{:S(2)}) async-start(bf16[512,2,3,2,128]{4,3,2,1,0:T(2,128)(2,1)} %copy.73), calls=%async_computation.1 | async-start | bytes 3145728 | tf_op jit(solution)/shard_map/all_to_all | solution.py:100
  408.9 2.7 copy-start.6
  408.9 2.7 copy-start.7
  411.6 1.2 copy-start.8
  411.6 1.5 copy-start.9
  413.1 1.2 copy-start.4
  413.2 1.5 copy-start.5
where the time goes:
time: 426 us
  other arithmetic  223 us (52%)
  local copies, waits for them, and re-layouts  75.7 us (18%)
  waiting for transfers between devices  61 us (14%)
  matrix products  52.3 us (12%)
  starting transfers between devices  11.1 us (3%)
    another operation x6, other arithmetic  120 us
    cos x2, other arithmetic, one_turn(): wave_re = jnp.cos(phases)[:, :, :, None, None, :]  63.9 us
    all_to_all x1, waiting for transfers between devices, on_device(): lax.all_to_all(green, 'freq', split_axis=1, concat_axis=0, tiled=True)  61 us
    dot_general x2, matrix products, one_turn(): jnp.einsum('rgkp,ghfscqp->rkhfscq', routed, weighted, preferred_element_t...  46.6 us
    convert_element_type x2, other arithmetic, one_turn(): tile = tiles_here[region_map[blocks]].astype(jnp.float32)  28.8 us
    mul x2, local copies, waits for them, and re-layouts, one_turn(): wave_re * tile_re - wave_im * tile_im  28.4 us
    gather x4, local copies, waits for them, and re-layouts, one_turn(): tile = tiles_here[region_map[blocks]].astype(jnp.float32)  15 us
    reshape x2, local copies, waits for them, and re-layouts, on_device(): return motion.reshape(row_count, site_count, C, wave_len)  9.76 us
  transfers between devices with their start and end apart: 2, of which 1 were waited for; matrix products, arithmetic and copies ran while one was open for 11% of the time, Pallas kernels for 0%

commit v1 on v0

--- a/solution.py
+++ b/solution.py
@@ -8,6 +8,17 @@
 C = 3
 TWO_PI = 2.0 * math.pi
 OUT_GAIN = 8.0
+
+
+def split_up(value, dim, size):
+    before, after = (value.shape[:dim], value.shape[dim + 1 :])
+    return jnp.moveaxis(value.reshape(*before, size, -1, *after), dim, 0)
+
+
+def joined_along(tiles, dim):
+    dims = list(tiles.shape[1:])
+    dims[dim] *= tiles.shape[0]
+    return jnp.moveaxis(tiles, 0, dim).reshape(dims)
 
 
 def on_device(
@@ -43,7 +54,14 @@
     group_size = math.gcd(slot_total, 32)
     turn_count = slot_total // group_size
     rupture_ids = jnp.arange(rupture_count, dtype=jnp.int32)
-    tiles_here = lax.all_to_all(green, "freq", split_axis=1, concat_axis=0, tiled=True)
+    size, mine = (lax.axis_size("freq"), lax.axis_index("freq"))
+    tiles = split_up(green, 1, size)
+    done = [tiles[mine]]
+    for step in range(1, size):
+        sent = tiles[(mine + step) % size]
+        done.append(lax.ppermute(sent, "freq", [(i, (i + step) % size) for i in range(size)]))
+    tiles = jnp.stack(done)[(mine - jnp.arange(size)) % size]
+    tiles_here = joined_along(tiles, 0)
     site_items = tiles_here.shape[2]
 
     def one_turn(turn_index, totals):

time: 426 us -> 429 us (level)
  waiting for transfers between devices: 61 us -> 24.9 us
  starting transfers between devices: 11.1 us -> 39.7 us
  local copies, waits for them, and re-layouts: 75.7 us -> 85.1 us
    all_to_all x1 -> x0, waiting for transfers between devices: 61 us -> none  [on_device(): lax.all_to_all(green, 'freq', split_axis=1, concat_axis=0, tiled=True)]
    ppermute x0 -> x7, waiting for transfers between devices: none -> 24.9 us  [on_device(): lax.ppermute(sent, 'freq', [(i, (i + step) % size) for i in range(size)])]
    all_to_all x1, starting transfers between devices: 3.64 us -> 24.5 us  [on_device(): lax.all_to_all(spectrum, 'freq', split_axis=0, concat_axis=4, tiled=True)]
    ppermute x0 -> x7, starting transfers between devices: none -> 15.2 us  [on_device(): lax.ppermute(sent, 'freq', [(i, (i + step) % size) for i in range(size)])]
    all_to_all x1 -> x0, starting transfers between devices: 7.44 us -> none  [on_device(): lax.all_to_all(green, 'freq', split_axis=1, concat_axis=0, tiled=True)]
    unnamed x38 -> x45, local copies, waits for them, and re-layouts: 5.76 us -> 10.7 us
  transfers between devices with their start and end apart: 2 -> 8, of which waited for: 1 -> 2; matrix products, arithmetic and copies ran while one was open for 11% -> 12% of each run, Pallas kernels for 0% -> 0%
where the time goes in v1:
time: 429 us; the launch traced here: 428 us
  other arithmetic  223 us (52%)
  local copies, waits for them, and re-layouts  85.1 us (20%)
  matrix products  52.3 us (12%)
  starting transfers between devices  39.7 us (9%)
  waiting for transfers between devices  24.9 us (6%)
    another operation x6, other arithmetic  120 us
    cos x2, other arithmetic, one_turn(): wave_re = jnp.cos(phases)[:, :, :, None, None, :]  63.9 us
    dot_general x2, matrix products, one_turn(): jnp.einsum('rgkp,ghfscqp->rkhfscq', routed, weighted, preferred_element_t...  46.6 us
    convert_element_type x2, other arithmetic, one_turn(): tile = tiles_here[region_map[blocks]].astype(jnp.float32)  28.9 us
    mul x2, local copies, waits for them, and re-layouts, one_turn(): wave_re * tile_re - wave_im * tile_im  28.3 us
    ppermute x7, waiting for transfers between devices, on_device(): lax.ppermute(sent, 'freq', [(i, (i + step) % size) for i in range(size)])  24.9 us
    all_to_all x1, starting transfers between devices, on_device(): lax.all_to_all(spectrum, 'freq', split_axis=0, concat_axis=4, tiled=True)  24.5 us
    ppermute x7, starting transfers between devices, on_device(): lax.ppermute(sent, 'freq', [(i, (i + step) % size) for i in range(size)])  15.2 us
  transfers between devices with their start and end apart: 8, of which 2 were waited for; matrix products, arithmetic and copies ran while one was open for 12% of the time, Pallas kernels for 0%

profile of v1, /device:TPU:0, one launch (start us, length us, event | category | flops | bytes accessed | tf_op | source)
XLA Modules:
  0.0 427.8 jit_solution(14357176411918231488)
XLA Ops:
  0.0 2.4 copy.75
  2.5 1.6 dynamic-slice_bitcast_fusion
  4.1 3.0 collective-permute-start
  7.0 1.6 collective-permute-start.1
  8.6 2.6 collective-permute-start.2
  11.2 1.2 collective-permute-start.3
  12.4 2.6 collective-permute-start.4
  15.1 0.7 fusion.82
  15.8 0.7 fusion.73
  16.6 5.1 %fusion.75 = pred[64]{0:T(512)(128)(4,1)S(1)} fusion(s32[]{:T(128)} %bitcast.2, s32[]{:T(128)} %bitcast.3, s32[]{:T(128)} %bitcast.4, s32[]{:T(128)} %bitcast.5, s32[]{:T(128)} %bitcast.6, s32[]{:T(128)} %bitcast.8, s32[]{:T(128)} %bitcast.7, s32[]{:T(128)} %bitcast.1), kind=kLoop, calls=%fused_computation.162 | loop fusion | flops 2048 | bytes 96 | tf_op jit(solution)/shard_map/lt | solution.py:53
  21.7 0.7 broadcast_compare_fusion
  22.4 2.1 all_gather.3
  24.7 1.4 collective-permute-start.5
  26.1 1.0 bitcast_dynamic-update-slice_fusion.7
  27.2 2.8 collective-permute-start.6
  30.0 1.0 bitcast_dynamic-update-slice_fusion.6
  31.1 22.3 %collective-permute-done.2 = bf16[1,128,2,3,2,128]{5,1,4,3,2,0:T(8,128)(2,1)} collective-permute-done((bf16[1,128,2,3,2,128]{5,1,4,3,2,0:T(8,128)(2,1)}, bf16[1,128,2,3,2,128]{5,1,4,3,2,0:T(8,128)(2,1)}, u32[]{:S(2)}, u32[]{:S(2)}) %collective-permute-start.2) | collective-permute-done | bytes 393248 | tf_op jit(solution)/shard_map/ppermute | solution.py:62
  53.4 1.0 bitcast_dynamic-update-slice_fusion.5
  54.4 1.0 bitcast_dynamic-update-slice_fusion.4
  55.5 1.0 bitcast_dynamic-update-slice_fusion.3
  56.6 2.6 collective-permute-done.6
  59.3 1.6 copy-done.2
  60.9 3.1 gather_fusion.7
  64.0 274.9 %while.14 = (s32[]{:T(128)}, f32[8,16,4,128,2,3,2]{3,1,6,5,4,2,0:T(8,128)}, s32[64]{0:T(128)S(1)}, pred[64]{0:T(512)(128)(4,1)S(1)}, s32[64]{0:T(128)S(1)}, /*in...) while((s32[]{:T(128)}, ...), condition=%wide.region_2.3_spmd.clone, body=%wide.region_0.2_spmd.clone.sunk | while | flops 6658150912 | bytes 280112832 | solution.py:99
  64.2 0.7 gather_fusion.1
  64.9 0.6 gather_fusion.2
  65.5 0.6 gather_fusion
  66.4 0.6 gather_fusion.3
  67.1 31.9 %multiply_cosine_fusion.2 = (f32[32,4,128,128]{3,2,0,1:T(8,128)}, f32[32,4,128,128]{3,2,0,1:T(8,128)}) fusion(f32[32,4,128]{2,0,1:T(8,128)S(1)} %sqrt_multiply_fusion.2, f32[128]{0:T(128)S(1)} %convert_multiply_fusion.3), kind=kLoop, calls=%fused_computation.17.clone.1 | loop fusion | flops 4194304 | bytes 16843264 | tf_op jit(solution)/shard_map/while/body/eval_jaxpr/cos | solution.py:80
  99.1 0.7 gather_fusion.4
  99.8 6.8 %gather_fusion.5 = bf16[32,128,2,3,2,128]{5,1,4,3,2,0:T(8,128)(2,1)} fusion(bf16[8,128,2,3,2,128]{5,1,4,3,2,0:T(8,128)(2,1)S(1)} %get-tuple-element.576, s32[1024]{0:T(1024)S(1)} %pad_clamp_fusion.9), kind=kCustom, calls=%fused_computation.6.clone.clone.1 | custom fusion | bytes 25165952 | tf_op jit(solution)/shard_map/while/body/eval_jaxpr/gather | solution.py:73
  106.6 14.5 %convert_element_type.116 = f32[32,128,2,3,2,128]{5,1,4,3,2,0:T(8,128)} convert(bf16[32,128,2,3,2,128]{5,1,4,3,2,0:T(8,128)(2,1)} %gather_fusion.5) | non-fusion elementwise | flops 6291456 | bytes 37748736 | tf_op jit(solution)/shard_map/while/body/eval_jaxpr/convert_element_type | solution.py:73
  121.1 14.2 %slice_bitcast_fusion.3 = (f32[32,128,2,3,128]{4,1,3,2,0:T(8,128)S(1)}, f32[32,128,2,3,128]{4,1,3,2,0:T(8,128)}) fusion(f32[32,128,2,3,2,128]{5,1,4,3,2,0:T(8,128)} %convert_element_type.116), kind=kLoop, calls=%fused_computation.15.clone.1 | loop fusion | bytes 50331648 | tf_op jit(solution)/shard_map/while/body/eval_jaxpr/mul | solution.py:85
  135.2 41.1 %subtract_convert_fusion.2 = (bf16[32,4,128,2,3,1,128]{6,2,0,5,4,3,1:T(8,128)(2,1)}, bf16[32,4,128,2,3,1,128]{6,2,0,5,4,3,1:T(8,128)(2,1)}) fusion(f32[32,4,128,128]{3,2,0,1:T(8,128)} %get-tuple-element.525, f32[32,4,128,128]{3,2,0,1:T(8,128)} %get-tuple-element.526, f32[32,128,2,3,128]{4,1,3,2,0:T(8,128)S(1)} %get-tuple-element.527, ...), kind=kLoop, calls=%fused_computation.12.clone.1 | loop fusion | flops 100663296 | bytes 92274688 | tf_op jit(solution)/shard_map/convert
  176.4 1.6 gather_fusion.6
  178.2 23.2 %bitcast_add_fusion.2 = f32[8,16,4,128,2,3,2]{3,1,6,5,4,2,0:T(8,128)} fusion(f32[8,16,4,128,2,3,2]{3,1,6,5,4,2,0:T(8,128)} %get-tuple-element.549, bf16[32,4,128,2,3,1,128]{6,2,0,5,4,3,1:T(8,128)(2,1)} %get-tuple-element.529, bf16[32,4,128,2,3,1,128]{6,2,0,5,4,3,1:T(8,128)(2,1)} %get-tuple-element.530, pred[]{:T(512)S(6)} %compare.117, ...), kind=kOutput, calls=%fused_computation.19.clone.1 | convolution fusion | flops 6546784256 | bytes 56754688 | tf_op jit(solution)/shard_map/while/body/eval_jaxpr/rgkp,ghfscqp->rkhfscq/dot_general | solution.py:91
  201.5 0.7 gather_fusion.1
  202.2 0.6 gather_fusion.2
  202.8 0.6 gather_fusion
  203.7 0.6 gather_fusion.3
  204.4 31.9 %multiply_cosine_fusion.2 = (f32[32,4,128,128]{3,2,0,1:T(8,128)}, f32[32,4,128,128]{3,2,0,1:T(8,128)}) fusion(f32[32,4,128]{2,0,1:T(8,128)S(1)} %sqrt_multiply_fusion.2, f32[128]{0:T(128)S(1)} %convert_multiply_fusion.3), kind=kLoop, calls=%fused_computation.17.clone.1 | loop fusion | flops 4194304 | bytes 16843264 | tf_op jit(solution)/shard_map/while/body/eval_jaxpr/cos | solution.py:80
  236.4 0.7 gather_fusion.4
  237.1 6.8 %gather_fusion.5 = bf16[32,128,2,3,2,128]{5,1,4,3,2,0:T(8,128)(2,1)} fusion(bf16[8,128,2,3,2,128]{5,1,4,3,2,0:T(8,128)(2,1)S(1)} %get-tuple-element.576, s32[1024]{0:T(1024)S(1)} %pad_clamp_fusion.9), kind=kCustom, calls=%fused_computation.6.clone.clone.1 | custom fusion | bytes 25165952 | tf_op jit(solution)/shard_map/while/body/eval_jaxpr/gather | solution.py:73
  243.9 14.5 %convert_element_type.116 = f32[32,128,2,3,2,128]{5,1,4,3,2,0:T(8,128)} convert(bf16[32,128,2,3,2,128]{5,1,4,3,2,0:T(8,128)(2,1)} %gather_fusion.5) | non-fusion elementwise | flops 6291456 | bytes 37748736 | tf_op jit(solution)/shard_map/while/body/eval_jaxpr/convert_element_type | solution.py:73
  258.3 14.2 %slice_bitcast_fusion.3 = (f32[32,128,2,3,128]{4,1,3,2,0:T(8,128)S(1)}, f32[32,128,2,3,128]{4,1,3,2,0:T(8,128)}) fusion(f32[32,128,2,3,2,128]{5,1,4,3,2,0:T(8,128)} %convert_element_type.116), kind=kLoop, calls=%fused_computation.15.clone.1 | loop fusion | bytes 50331648 | tf_op jit(solution)/shard_map/while/body/eval_jaxpr/mul | solution.py:85
  272.5 41.1 %subtract_convert_fusion.2 = (bf16[32,4,128,2,3,1,128]{6,2,0,5,4,3,1:T(8,128)(2,1)}, bf16[32,4,128,2,3,1,128]{6,2,0,5,4,3,1:T(8,128)(2,1)}) fusion(f32[32,4,128,128]{3,2,0,1:T(8,128)} %get-tuple-element.525, f32[32,4,128,128]{3,2,0,1:T(8,128)} %get-tuple-element.526, f32[32,128,2,3,128]{4,1,3,2,0:T(8,128)S(1)} %get-tuple-element.527, ...), kind=kLoop, calls=%fused_computation.12.clone.1 | loop fusion | flops 100663296 | bytes 92274688 | tf_op jit(solution)/shard_map/convert
  313.6 1.6 gather_fusion.6
  315.5 23.5 %bitcast_add_fusion.2 = f32[8,16,4,128,2,3,2]{3,1,6,5,4,2,0:T(8,128)} fusion(f32[8,16,4,128,2,3,2]{3,1,6,5,4,2,0:T(8,128)} %get-tuple-element.549, bf16[32,4,128,2,3,1,128]{6,2,0,5,4,3,1:T(8,128)(2,1)} %get-tuple-element.529, bf16[32,4,128,2,3,1,128]{6,2,0,5,4,3,1:T(8,128)(2,1)} %get-tuple-element.530, pred[]{:T(512)S(6)} %compare.117, ...), kind=kOutput, calls=%fused_computation.19.clone.1 | convolution fusion | flops 6546784256 | bytes 56754688 | tf_op jit(solution)/shard_map/while/body/eval_jaxpr/rgkp,ghfscqp->rkhfscq/dot_general | solution.py:91
  338.9 2.4 multiply_subtract_fusion
  341.7 2.0 copy.79
  343.7 2.8 copy.80
  346.5 24.5 %all-to-all-start = ((bf16[512,2,3,2,128]{4,3,2,1,0:T(2,128)(2,1)}), bf16[512,2,3,2,128]{4,3,2,1,0:T(2,128)(2,1)S(1)}, u32[]{:S(2)}, u32[]{:S(2)}) async-start(bf16[512,2,3,2,128]{4,3,2,1,0:T(2,128)(2,1)} %copy.80), calls=%async_computation | async-start | bytes 3145728 | tf_op jit(solution)/shard_map/all_to_all | solution.py:118
  371.0 9.3 %negate_convert_fusion.3 = (bf16[1024,512]{1,0:T(8,128)(2,1)}, bf16[1024,512]{1,0:T(8,128)(2,1)}) fusion(), kind=kLoop, calls=%fused_computation.98 | loop fusion | flops 8912896 | bytes 2097152 | tf_op jit(solution)/shard_map/convert.9
  380.3 9.4 %cosine_convert_fusion.1 = (bf16[1024,512]{1,0:T(8,128)(2,1)}, bf16[1024,512]{1,0:T(8,128)(2,1)}) fusion(s32[512]{0:T(512)S(1)} %iota_add_fusion.1), kind=kLoop, calls=%fused_computation.91 | loop fusion | flops 8912896 | bytes 2099200 | tf_op jit(solution)/shard_map/convert.4
  389.6 9.4 %cosine_convert_fusion.2 = (bf16[1024,512]{1,0:T(8,128)(2,1)}, bf16[1024,512]{1,0:T(8,128)(2,1)}) fusion(s32[512]{0:T(512)S(1)} %iota_add_fusion.2), kind=kLoop, calls=%fused_computation.95 | loop fusion | flops 8912896 | bytes 2099200 | tf_op jit(solution)/shard_map/convert.6
  399.0 9.3 %cosine_convert_fusion = (bf16[1024,512]{1,0:T(8,128)(2,1)}, bf16[1024,512]{1,0:T(8,128)(2,1)}) fusion(s32[512]{0:T(512)S(1)} %iota_add_fusion), kind=kLoop, calls=%fused_computation.87 | loop fusion | flops 8912896 | bytes 2099200 | tf_op jit(solution)/shard_map/convert.2
  408.3 1.8 copy.91
  410.2 0.7 reshape.259
  410.9 2.7 fusion.62
  413.6 1.0 fusion.65
  415.2 1.0 fusion.68
  416.7 1.0 fusion.59
  418.0 3.0 reshape.260
  421.0 6.8 %copy.82 = f32[64,2,3,2048]{3,1,2,0:T(2,128)} copy(f32[64,2,3,2048]{3,2,1,0:T(4,128)} %reshape.260) | data formatting | bytes 6291456 | tf_op jit(solution)/shard_map/reshape | solution.py:137
  (89 shorter events, 3.7 us)
Async XLA Ops:
  2.4 12.7 %copy-start.11 = (s32[8]{0:T(128)S(1)}, s32[8]{0:T(128)}, u32[]{:S(2)}) copy-start(s32[8]{0:T(128)} %param.19) | copy-start | bytes 100
  2.4 13.3 %copy-start.10 = (bf16[8,8,8,128]{3,2,1,0:T(8,128)(2,1)S(1)}, bf16[8,8,8,128]{3,2,1,0:T(8,128)(2,1)}, u32[]{:S(2)}) copy-start(bf16[8,8,8,128]{3,2,1,0:T(8,128)(2,1)} %param.13) | copy-start | bytes 393220
  2.5 13.4 %copy-start.14 = (f32[8,16]{1,0:T(8,128)S(1)}, f32[8,16]{1,0:T(8,128)}, u32[]{:S(2)}) copy-start(f32[8,16]{1,0:T(8,128)} %param.17) | copy-start | bytes 1540
  2.5 19.2 %copy-start.16 = (s32[8]{0:T(128)S(1)}, s32[8]{0:T(128)}, u32[]{:S(2)}) copy-start(s32[8]{0:T(128)} %param.20) | copy-start | bytes 100
  2.5 22.0 %copy-start.13 = (f32[8,4,3]{0,1,2:T(4,128)S(1)}, f32[8,4,3]{0,1,2:T(4,128)}, u32[]{:S(2)}) copy-start(f32[8,4,3]{0,1,2:T(4,128)} %param.15) | copy-start | bytes 1156
  2.5 22.1 %copy-start.15 = (f32[8,4]{0,1:T(4,128)S(1)}, f32[8,4]{0,1:T(4,128)}, u32[]{:S(2)}) copy-start(f32[8,4]{0,1:T(4,128)} %param.16) | copy-start | bytes 388
  4.1 20.7 %collective-permute-start = (bf16[1,128,2,3,2,128]{5,1,4,3,2,0:T(8,128)(2,1)}, bf16[1,128,2,3,2,128]{5,1,4,3,2,0:T(8,128)(2,1)}, u32[]{:S(2)}, u32[]{:S(2)}) collective-permute-start(bf16[1,128,2,3,2,128]{5,1,4,3,2,0:T(8,128)(2,1)} %get-tuple-element.415), channel_id=1, source_target_pairs={{0,2},{2,4},{4,6},{6,8},{8,10},{10,12},{12,14},{14,0},{1,3},{3,5},... | collective-permute-start | bytes 1179656 | tf_op jit(solution)/shard_map/ppermute | solution.py:62
  7.0 20.2 %collective-permute-start.1 = (bf16[1,128,2,3,2,128]{5,1,4,3,2,0:T(8,128)(2,1)}, bf16[1,128,2,3,2,128]{5,1,4,3,2,0:T(8,128)(2,1)}, u32[]{:S(2)}, u32[]{:S(2)}) collective-permute-start(bf16[1,128,2,3,2,128]{5,1,4,3,2,0:T(8,128)(2,1)} %get-tuple-element.414), channel_id=1, source_target_pairs={{0,4},{2,6},{4,8},{6,10},{8,12},{10,14},{12,0},{14,2},{1,5},{3,7},... | collective-permute-start | bytes 1179656 | tf_op jit(solution)/shard_map/ppermute | solution.py:62
  8.6 44.7 %collective-permute-start.2 = (bf16[1,128,2,3,2,128]{5,1,4,3,2,0:T(8,128)(2,1)}, bf16[1,128,2,3,2,128]{5,1,4,3,2,0:T(8,128)(2,1)}, u32[]{:S(2)}, u32[]{:S(2)}) collective-permute-start(bf16[1,128,2,3,2,128]{5,1,4,3,2,0:T(8,128)(2,1)} %get-tuple-element.413), channel_id=1, source_target_pairs={{0,6},{2,8},{4,10},{6,12},{8,14},{10,0},{12,2},{14,4},{1,7},{3,9},... | collective-permute-start | bytes 1179656 | tf_op jit(solution)/shard_map/ppermute | solution.py:62
  11.2 43.2 %collective-permute-start.3 = (bf16[1,128,2,3,2,128]{5,1,4,3,2,0:T(8,128)(2,1)}, bf16[1,128,2,3,2,128]{5,1,4,3,2,0:T(8,128)(2,1)}, u32[]{:S(2)}, u32[]{:S(2)}) collective-permute-start(bf16[1,128,2,3,2,128]{5,1,4,3,2,0:T(8,128)(2,1)} %get-tuple-element.412), channel_id=1, source_target_pairs={{0,8},{2,10},{4,12},{6,14},{8,0},{10,2},{12,4},{14,6},{1,9},{3,11}... | collective-permute-start | bytes 1179656 | tf_op jit(solution)/shard_map/ppermute | solution.py:62
  12.4 43.1 %collective-permute-start.4 = (bf16[1,128,2,3,2,128]{5,1,4,3,2,0:T(8,128)(2,1)}, bf16[1,128,2,3,2,128]{5,1,4,3,2,0:T(8,128)(2,1)}, u32[]{:S(2)}, u32[]{:S(2)}) collective-permute-start(bf16[1,128,2,3,2,128]{5,1,4,3,2,0:T(8,128)(2,1)} %get-tuple-element.411), channel_id=1, source_target_pairs={{0,10},{2,12},{4,14},{6,0},{8,2},{10,4},{12,6},{14,8},{1,11},{3,13... | collective-permute-start | bytes 1179656 | tf_op jit(solution)/shard_map/ppermute | solution.py:62
  24.7 31.8 %collective-permute-start.5 = (bf16[1,128,2,3,2,128]{5,1,4,3,2,0:T(8,128)(2,1)}, bf16[1,128,2,3,2,128]{5,1,4,3,2,0:T(8,128)(2,1)S(1)}, u32[]{:S(2)}, u32[]{:S(2)}) collective-permute-start(bf16[1,128,2,3,2,128]{5,1,4,3,2,0:T(8,128)(2,1)} %get-tuple-element.410), channel_id=1, source_target_pairs={{0,12},{2,14},{4,0},{6,2},{8,4},{10,6},{12,8},{14,10},{1,13},{3,15... | collective-permute-start | bytes 1179656 | tf_op jit(solution)/shard_map/ppermute | solution.py:62
  27.2 32.0 %collective-permute-start.6 = (bf16[1,128,2,3,2,128]{5,1,4,3,2,0:T(8,128)(2,1)}, bf16[1,128,2,3,2,128]{5,1,4,3,2,0:T(8,128)(2,1)S(1)}, u32[]{:S(2)}, u32[]{:S(2)}) collective-permute-start(bf16[1,128,2,3,2,128]{5,1,4,3,2,0:T(8,128)(2,1)} %get-tuple-element.409), channel_id=1, source_target_pairs={{0,14},{2,0},{4,2},{6,4},{8,6},{10,8},{12,10},{14,12},{1,15},{3,1}... | collective-permute-start | bytes 1179656 | tf_op jit(solution)/shard_map/ppermute | solution.py:62
  59.3 1.6 copy-start.2
  60.9 3.1 copy-start
  60.9 3.1 copy-start.1
  60.9 3.1 copy-start.3
  338.9 2.4 copy-start.12
  346.5 61.8 %all-to-all-start = ((bf16[512,2,3,2,128]{4,3,2,1,0:T(2,128)(2,1)}), bf16[512,2,3,2,128]{4,3,2,1,0:T(2,128)(2,1)S(1)}, u32[]{:S(2)}, u32[]{:S(2)}) async-start(bf16[512,2,3,2,128]{4,3,2,1,0:T(2,128)(2,1)} %copy.80), calls=%async_computation | async-start | bytes 3145728 | tf_op jit(solution)/shard_map/all_to_all | solution.py:118
  410.9 2.7 copy-start.6
  410.9 2.7 copy-start.7
  413.6 1.2 copy-start.8
  413.6 1.5 copy-start.9
  415.2 1.2 copy-start.4
  415.2 1.5 copy-start.5
